TPU v7x, 128 devices: a whole 4x4x4 slice. The times are simulated.
128 devices in a mesh: ctx: 16 (over x_hi, z, core), head: 8 (over x_lo, y).
Axes of the slice: x: 4 (x_hi: 2, x_lo: 2; x = x_hi * 2 + x_lo), y: 4, z: 4, core: 2. Of those that a mesh axis runs over, the one named last changes fastest.
Arguments:
- queries: bfloat16 [2, 24576, 4096], P(None, 'ctx', 'head')
- layer_keys_input: bfloat16 [2, 24576, 2048], P(None, 'ctx', 'head')
- layer_values_input: bfloat16 [2, 24576, 2048], P(None, 'ctx', 'head')
- attn_out: bfloat16 [2, 24576, 4096], P(None, 'ctx', 'head'), as said below
- grad_out: bfloat16 [2, 24576, 4096], P(None, 'ctx', 'head'), may hold values from -6 to 6
- log_norm: float32 [2, 32, 24576], P(None, 'head', 'ctx'), as said below
- window: int32 [2], replicated, may hold values from 512 to 1024, as said below
Outputs:
- grad_query: bfloat16 [2, 24576, 4096], P(None, ('ctx', 'head'))
- grad_key: bfloat16 [2, 24576, 2048], P(None, ('ctx', 'head'))
- grad_value: bfloat16 [2, 24576, 2048], P(None, ('ctx', 'head'))
Inputs may be any that keep to these rules, and one draw needn't show every extreme that they name: Each layer's window is 512 to 1024 tokens; one of the layers has exactly 1024. log_norm is the log of the sum, over each query's window, of exp of its scaled scores against layer_keys_input. attn_out is the attention output that these weights give from layer_values_input.
All inputs are finite; a program needn't handle non-finite values.
Results may differ from a plain program's by a relative error of at most 0.005.
Values may be sent and summed in bfloat16 or wider, within the bound.
A program may use at most 256 MiB of HBM per device.

v0:
```python
import jax
import jax.numpy as jnp
from jax import lax
from jax.sharding import PartitionSpec as P

HEAD_SIZE = 128
WINDOW_LENGTH = 1024
QUERY_PRE = 168
SLIDING_LAYERS = 2
BLOCK = 512


def shifted(value, axis, steps):
    count = lax.axis_size(axis)
    first, last = (max(0, -steps), min(count, count - steps))
    return lax.ppermute(value, axis, [(source, source + steps) for source in range(first, last)])


def block_grads(q_block, do_block, lse_block, dlt_block, k_block, v_block, q_pos, k_pos, win):
    row_count, head_count, head_dim = q_block.shape
    kv_count = k_block.shape[1]
    query_group_count = head_count // kv_count
    score_scale = QUERY_PRE ** (-0.5)
    query_head_count = q_block.reshape(row_count, kv_count, query_group_count, head_dim)
    do_heads = do_block.reshape(row_count, kv_count, query_group_count, head_dim)
    scores = (
        jnp.einsum("rkgd,ckd->kgrc", query_head_count, k_block, preferred_element_type=jnp.float32)
        * score_scale
    )
    lse_heads = lse_block.reshape(kv_count, query_group_count, row_count)
    dlt_heads = dlt_block.reshape(kv_count, query_group_count, row_count)
    visible = (
        (k_pos[None, :] <= q_pos[:, None])
        & (q_pos[:, None] - k_pos[None, :] < win)
        & (k_pos[None, :] >= 0)
    )
    attn_prob = jnp.where(visible, jnp.exp(scores - lse_heads[..., None]), 0.0)
    prob_low = attn_prob.astype(jnp.bfloat16)
    grad_prob = jnp.einsum("rkgd,ckd->kgrc", do_heads, v_block, preferred_element_type=jnp.float32)
    grad_score = attn_prob * (grad_prob - dlt_heads[..., None])
    score_low = grad_score.astype(jnp.bfloat16)
    dv_part = jnp.einsum("kgrc,rkgd->ckd", prob_low, do_heads, preferred_element_type=jnp.float32)
    dk_part = (
        jnp.einsum(
            "kgrc,rkgd->ckd", score_low, query_head_count, preferred_element_type=jnp.float32
        )
        * score_scale
    )
    dq_part = (
        jnp.einsum("kgrc,ckd->rkgd", score_low, k_block, preferred_element_type=jnp.float32)
        * score_scale
    )
    return (dq_part.reshape(row_count, head_count, head_dim), dk_part, dv_part)


def sweep_blocks(lower, upper, state, layer_parts, offset_tok):
    q_all, do_all, lse_all, dlt_all, k_ext, v_ext, win = layer_parts

    def step(block_idx, carry):
        dq_all, key_gradient_total, value_gradient_total = carry
        start_row = block_idx * BLOCK
        q_block = lax.dynamic_slice_in_dim(q_all, start_row, BLOCK, 0)
        do_block = lax.dynamic_slice_in_dim(do_all, start_row, BLOCK, 0)
        lse_block = lax.dynamic_slice_in_dim(lse_all, start_row, BLOCK, 1)
        dlt_block = lax.dynamic_slice_in_dim(dlt_all, start_row, BLOCK, 1)
        k_block = lax.dynamic_slice_in_dim(k_ext, start_row, WINDOW_LENGTH + BLOCK, 0)
        v_block = lax.dynamic_slice_in_dim(v_ext, start_row, WINDOW_LENGTH + BLOCK, 0)
        q_pos = offset_tok + start_row + jnp.arange(BLOCK, dtype=jnp.int32)
        k_pos = (
            offset_tok
            + start_row
            - WINDOW_LENGTH
            + jnp.arange(WINDOW_LENGTH + BLOCK, dtype=jnp.int32)
        )
        dq_part, dk_part, dv_part = block_grads(
            q_block, do_block, lse_block, dlt_block, k_block, v_block, q_pos, k_pos, win
        )
        dq_all = lax.dynamic_update_slice_in_dim(dq_all, dq_part.astype(jnp.bfloat16), start_row, 0)
        dk_old = lax.dynamic_slice_in_dim(key_gradient_total, start_row, WINDOW_LENGTH + BLOCK, 0)
        dv_old = lax.dynamic_slice_in_dim(value_gradient_total, start_row, WINDOW_LENGTH + BLOCK, 0)
        key_gradient_total = lax.dynamic_update_slice_in_dim(
            key_gradient_total, dk_old + dk_part, start_row, 0
        )
        value_gradient_total = lax.dynamic_update_slice_in_dim(
            value_gradient_total, dv_old + dv_part, start_row, 0
        )
        return (dq_all, key_gradient_total, value_gradient_total)

    if upper <= lower:
        return state
    return lax.fori_loop(lower, upper, step, state)


def send_back(states, tok_local):
    halo_dk = jnp.stack([entry[1][:WINDOW_LENGTH] for entry in states], 0)
    halo_dv = jnp.stack([entry[2][:WINDOW_LENGTH] for entry in states], 0)
    back_dk, back_dv = shifted((halo_dk, halo_dv), "ctx", -1)
    result = []
    for layer_number in range(len(states)):
        dq_all, key_gradient_total, value_gradient_total = states[layer_number]
        key_gradient_total = key_gradient_total.at[tok_local:].add(back_dk[layer_number])
        value_gradient_total = value_gradient_total.at[tok_local:].add(back_dv[layer_number])
        result.append((dq_all, key_gradient_total, value_gradient_total))
    return result


def shards(queries, layer_keys_input, layer_values_input, attn_out, grad_out, log_norm, window):
    tok_local = queries.shape[1]
    head_local = log_norm.shape[1]
    kv_local = layer_keys_input.shape[2] // HEAD_SIZE
    offset_tok = lax.axis_index("ctx") * tok_local
    delta = jnp.sum(
        (grad_out.astype(jnp.float32) * attn_out.astype(jnp.float32)).reshape(
            SLIDING_LAYERS, tok_local, head_local, HEAD_SIZE
        ),
        axis=-1,
    ).transpose(0, 2, 1)
    rim_keys, rim_values = shifted(
        (
            layer_keys_input[:, tok_local - WINDOW_LENGTH :],
            layer_values_input[:, tok_local - WINDOW_LENGTH :],
        ),
        "ctx",
        1,
    )
    all_parts = []
    states = []
    for layer_number in range(SLIDING_LAYERS):
        k_ext = jnp.concatenate(
            [rim_keys[layer_number], layer_keys_input[layer_number]], 0
        ).reshape(WINDOW_LENGTH + tok_local, kv_local, HEAD_SIZE)
        v_ext = jnp.concatenate(
            [rim_values[layer_number], layer_values_input[layer_number]], 0
        ).reshape(WINDOW_LENGTH + tok_local, kv_local, HEAD_SIZE)
        all_parts.append(
            (
                queries[layer_number].reshape(tok_local, head_local, HEAD_SIZE),
                grad_out[layer_number].reshape(tok_local, head_local, HEAD_SIZE),
                log_norm[layer_number],
                delta[layer_number],
                k_ext,
                v_ext,
                window[layer_number],
            )
        )
        states.append(
            (
                jnp.zeros((tok_local, head_local, HEAD_SIZE), jnp.bfloat16),
                jnp.zeros((WINDOW_LENGTH + tok_local, kv_local, HEAD_SIZE), jnp.float32),
                jnp.zeros((WINDOW_LENGTH + tok_local, kv_local, HEAD_SIZE), jnp.float32),
            )
        )
    block_count = tok_local // BLOCK
    for layer_number in range(SLIDING_LAYERS):
        states[layer_number] = sweep_blocks(
            0, block_count, states[layer_number], all_parts[layer_number], offset_tok
        )
    states = send_back(states, tok_local)
    for layer_number in range(SLIDING_LAYERS):
        states[layer_number] = sweep_blocks(
            block_count, block_count, states[layer_number], all_parts[layer_number], offset_tok
        )
    dq_stack = jnp.stack(
        [entry[0].reshape(tok_local, head_local * HEAD_SIZE) for entry in states], 0
    )
    dk_stack = jnp.stack(
        [
            entry[1][WINDOW_LENGTH:].astype(jnp.bfloat16).reshape(tok_local, kv_local * HEAD_SIZE)
            for entry in states
        ],
        0,
    )
    dv_stack = jnp.stack(
        [
            entry[2][WINDOW_LENGTH:].astype(jnp.bfloat16).reshape(tok_local, kv_local * HEAD_SIZE)
            for entry in states
        ],
        0,
    )
    grad_query, grad_key, grad_value = (
        lax.all_to_all(dq_stack, "head", split_axis=1, concat_axis=2, tiled=True),
        lax.all_to_all(dk_stack, "head", split_axis=1, concat_axis=2, tiled=True),
        lax.all_to_all(dv_stack, "head", split_axis=1, concat_axis=2, tiled=True),
    )
    return (grad_query, grad_key, grad_value)


def solution(mesh):
    in_specs = (
        P(None, "ctx", "head"),
        P(None, "ctx", "head"),
        P(None, "ctx", "head"),
        P(None, "ctx", "head"),
        P(None, "ctx", "head"),
        P(None, "head", "ctx"),
        P(),
    )
    out_specs = (
        P(None, ("ctx", "head"), None),
        P(None, ("ctx", "head"), None),
        P(None, ("ctx", "head"), None),
    )
    return jax.shard_map(shards, mesh=mesh, in_specs=in_specs, out_specs=out_specs, check_vma=False)
```

profile of v0, /device:TPU:6, one launch (start us, length us, event | category | flops | bytes accessed | tf_op | source)
XLA Modules:
  0.0 417.6 jit_solution(7210230822365985322)
XLA Ops:
  3.2 2.0 collective-permute-start
  6.6 4.2 %collective-permute-start.1 = (bf16[2,1024,256]{1,2,0:T(8,128)(2,1)}, bf16[2,1024,256]{1,2,0:T(8,128)(2,1)}, u32[]{:S(2)}, u32[]{:S(2)}) collective-permute-start(bf16[2,1024,256]{1,2,0:T(8,128)(2,1)} %copy.217), channel_id=1, source_target_pairs={{0,8},{8,16},{16,24},{24,32},{32,40},{40,48},{48,56},{56,64},{64,7... | collective-permute-start | bytes 3145736 | tf_op jit(solution)/shard_map/ppermute | solution.py:16
  18.3 3.6 convert_multiply_fusion
  21.8 7.6 %reshape.250 = f32[2,1536,4,128]{3,2,1,0:T(4,128)} reshape(f32[2,1536,512]{2,1,0:T(8,128)} %convert_multiply_fusion) | data formatting | bytes 12582912 | tf_op jit(solution)/shard_map/reshape | solution.py:113
  29.4 7.3 %reduce_sum.9 = f32[2,1536,4]{2,1,0:T(8,128)} reduce(f32[2,1536,4,128]{3,2,1,0:T(4,128)} %reshape.250, f32[]{:T(128)} %constant.258.clone.1), dimensions={3}, to_apply=%region_0.0 | reduce | flops 1560576 | bytes 6340612 | tf_op jit(solution)/shard_map/reduce_sum | solution.py:112
  36.7 2.7 slice_bitcast_fusion.9
  39.4 2.3 copy.220
  41.7 2.3 copy.222
  44.0 2.6 copy.221
  46.6 2.6 copy.223
  50.6 2.3 copy.215
  52.9 2.3 copy.218
  60.5 2.1 fusion.85
  62.6 2.1 fusion.84
  67.9 1.8 broadcast.211.clone.1
  69.7 98.0 %while.43 = (s32[]{:T(128)}, bf16[1536,4,128]{0,2,1:T(8,128)(2,1)}, f32[2560,2,128]{0,2,1:T(8,128)S(1)}, f32[2560,2,128]{0,2,1:T(8,128)}, bf16[2560,2,128]{0,2,1...) while((s32[]{:T(128)}, bf16[1536,4,128]{0,2,1:T(8,128)(2,1)}, ...), condition=%wide.region_4.5_spmd, body=%wide.region_3.4_spmd.sunk | while | flops 4063630336 | bytes 101821872 | solution.py:91
  69.7 2.1 constant_dynamic-slice_fusion.14
  71.8 7.5 %fusion.157 = f32[2,1536,512,2]{2,1,3,0:T(8,128)} fusion(bf16[512,2,2,128]{0,3,2,1:T(8,128)(2,1)S(1)} %bitcast.312, bf16[2560,2,128]{0,2,1:T(8,128)(2,1)} %get-tuple-element.1013, s32[]{:T(128)S(6)} %select_n.118), kind=kOutput, calls=%fused_computation.64.clone.1 | convolution fusion | flops 805306368 | bytes 13893636 | tf_op jit(solution)/shard_map/while/body/eval_jaxpr/rkgd,ckd->kgrc/dot_general | solution.py:27
  81.2 9.3 %fusion.159 = bf16[2,2,512,1536]{2,3,1,0:T(8,128)(2,1)S(1)} fusion(f32[2,1536,512,2]{2,1,3,0:T(8,128)} %fusion.157, bf16[512,2,2,128]{0,3,2,1:T(8,128)(2,1)} %bitcast.318, f32[2,2,512]{2,1,0:T(2,128)S(1)} %sub.283, f32[2,2,512]{2,1,0:T(2,128)S(1)} %sub.284, pred[512,1536]{0,1:T(8,128)(4,1)S(1)} %fusion.158, ...), kind=kOutput, calls=%fused_computation.44.clone.1 | convolution fusion | flops 824180736 | bytes 20987908 | tf_op jit(solution)/shard_map/while/body/eval_jaxpr/rkgd,ckd->kgrc/dot_general | solution.py:39
  92.3 2.3 fusion.161
  94.6 6.3 %fusion.162 = f32[2560,2,128]{0,2,1:T(8,128)S(1)} fusion(f32[2560,2,128]{0,2,1:T(8,128)S(1)} %copy-done.10, s32[]{:T(128)S(6)} %select_n.118, bf16[512,2,2,128]{0,3,2,1:T(8,128)(2,1)S(1)} %bitcast.319, f32[2,1536,512,2]{2,1,3,0:T(8,128)} %fusion.157, f32[2,2,512]{2,1,0:T(2,128)S(1)} %sub.284, pred[512,1536]{0,1:T(8,128)(4,1)S(1)} %fusion.158), kind=kOutput, calls=%fused_computation.56.clone.1 | convolution fusion | flops 818282496 | bytes 17047556 | tf_op jit(solution)/shard_map/while/body/eval_jaxpr/kgrc,rkgd->ckd/dot_general | solution.py:42
  102.4 2.1 constant_dynamic-slice_fusion.14
  104.5 7.5 %fusion.157 = f32[2,1536,512,2]{2,1,3,0:T(8,128)} fusion(bf16[512,2,2,128]{0,3,2,1:T(8,128)(2,1)S(1)} %bitcast.312, bf16[2560,2,128]{0,2,1:T(8,128)(2,1)} %get-tuple-element.1013, s32[]{:T(128)S(6)} %select_n.118), kind=kOutput, calls=%fused_computation.64.clone.1 | convolution fusion | flops 805306368 | bytes 13893636 | tf_op jit(solution)/shard_map/while/body/eval_jaxpr/rkgd,ckd->kgrc/dot_general | solution.py:27
  113.8 9.3 %fusion.159 = bf16[2,2,512,1536]{2,3,1,0:T(8,128)(2,1)S(1)} fusion(f32[2,1536,512,2]{2,1,3,0:T(8,128)} %fusion.157, bf16[512,2,2,128]{0,3,2,1:T(8,128)(2,1)} %bitcast.318, f32[2,2,512]{2,1,0:T(2,128)S(1)} %sub.283, f32[2,2,512]{2,1,0:T(2,128)S(1)} %sub.284, pred[512,1536]{0,1:T(8,128)(4,1)S(1)} %fusion.158, ...), kind=kOutput, calls=%fused_computation.44.clone.1 | convolution fusion | flops 824180736 | bytes 20987908 | tf_op jit(solution)/shard_map/while/body/eval_jaxpr/rkgd,ckd->kgrc/dot_general | solution.py:39
  125.0 2.3 fusion.161
  127.3 6.3 %fusion.162 = f32[2560,2,128]{0,2,1:T(8,128)S(1)} fusion(f32[2560,2,128]{0,2,1:T(8,128)S(1)} %copy-done.10, s32[]{:T(128)S(6)} %select_n.118, bf16[512,2,2,128]{0,3,2,1:T(8,128)(2,1)S(1)} %bitcast.319, f32[2,1536,512,2]{2,1,3,0:T(8,128)} %fusion.157, f32[2,2,512]{2,1,0:T(2,128)S(1)} %sub.284, pred[512,1536]{0,1:T(8,128)(4,1)S(1)} %fusion.158), kind=kOutput, calls=%fused_computation.56.clone.1 | convolution fusion | flops 818282496 | bytes 17047556 | tf_op jit(solution)/shard_map/while/body/eval_jaxpr/kgrc,rkgd->ckd/dot_general | solution.py:42
  135.1 2.1 constant_dynamic-slice_fusion.14
  137.1 7.5 %fusion.157 = f32[2,1536,512,2]{2,1,3,0:T(8,128)} fusion(bf16[512,2,2,128]{0,3,2,1:T(8,128)(2,1)S(1)} %bitcast.312, bf16[2560,2,128]{0,2,1:T(8,128)(2,1)} %get-tuple-element.1013, s32[]{:T(128)S(6)} %select_n.118), kind=kOutput, calls=%fused_computation.64.clone.1 | convolution fusion | flops 805306368 | bytes 13893636 | tf_op jit(solution)/shard_map/while/body/eval_jaxpr/rkgd,ckd->kgrc/dot_general | solution.py:27
  146.5 9.3 %fusion.159 = bf16[2,2,512,1536]{2,3,1,0:T(8,128)(2,1)S(1)} fusion(f32[2,1536,512,2]{2,1,3,0:T(8,128)} %fusion.157, bf16[512,2,2,128]{0,3,2,1:T(8,128)(2,1)} %bitcast.318, f32[2,2,512]{2,1,0:T(2,128)S(1)} %sub.283, f32[2,2,512]{2,1,0:T(2,128)S(1)} %sub.284, pred[512,1536]{0,1:T(8,128)(4,1)S(1)} %fusion.158, ...), kind=kOutput, calls=%fused_computation.44.clone.1 | convolution fusion | flops 824180736 | bytes 20987908 | tf_op jit(solution)/shard_map/while/body/eval_jaxpr/rkgd,ckd->kgrc/dot_general | solution.py:39
  157.7 2.3 fusion.161
  159.9 6.3 %fusion.162 = f32[2560,2,128]{0,2,1:T(8,128)S(1)} fusion(f32[2560,2,128]{0,2,1:T(8,128)S(1)} %copy-done.10, s32[]{:T(128)S(6)} %select_n.118, bf16[512,2,2,128]{0,3,2,1:T(8,128)(2,1)S(1)} %bitcast.319, f32[2,1536,512,2]{2,1,3,0:T(8,128)} %fusion.157, f32[2,2,512]{2,1,0:T(2,128)S(1)} %sub.284, pred[512,1536]{0,1:T(8,128)(4,1)S(1)} %fusion.158), kind=kOutput, calls=%fused_computation.56.clone.1 | convolution fusion | flops 818282496 | bytes 17047556 | tf_op jit(solution)/shard_map/while/body/eval_jaxpr/kgrc,rkgd->ckd/dot_general | solution.py:42
  167.7 4.4 %pad_maximum_fusion.5 = (bf16[2560,2,128]{0,2,1:T(8,128)(2,1)}, bf16[2560,2,128]{0,2,1:T(8,128)(2,1)}) fusion(bf16[1536,2,128]{0,2,1:T(8,128)(2,1)} %bitcast.332, bf16[1024,2,128]{0,2,1:T(8,128)(2,1)} %bitcast.341, bf16[1536,2,128]{0,2,1:T(8,128)(2,1)} %bitcast.333, bf16[1024,2,128]{0,2,1:T(8,128)(2,1)} %bitcast.342), kind=kLoop, calls=%fused_computation.94 | loop fusion | flops 5242880 | bytes 5242880 | tf_op jit(solution)/shard_map/concatenate | solution.py:129
  173.6 1.8 broadcast.211.clone.3
  175.5 98.3 %while.42 = (s32[]{:T(128)}, bf16[1536,4,128]{0,2,1:T(8,128)(2,1)}, f32[2560,2,128]{0,2,1:T(8,128)S(1)}, f32[2560,2,128]{0,2,1:T(8,128)}, bf16[2560,2,128]{0,2,1...) while((s32[]{:T(128)}, bf16[1536,4,128]{0,2,1:T(8,128)(2,1)}, ...), condition=%wide.region_2.3_spmd, body=%wide.region_1.2_spmd.sunk | while | flops 4063630336 | bytes 101821872 | solution.py:91
  175.5 2.1 constant_dynamic-slice_fusion.12
  177.6 7.5 %fusion.141 = f32[2,1536,512,2]{2,1,3,0:T(8,128)} fusion(bf16[512,2,2,128]{0,3,2,1:T(8,128)(2,1)S(1)} %bitcast.314, bf16[2560,2,128]{0,2,1:T(8,128)(2,1)} %get-tuple-element.1067, s32[]{:T(128)S(6)} %select_n.114), kind=kOutput, calls=%fused_computation.22.clone.1 | convolution fusion | flops 805306368 | bytes 13893636 | tf_op jit(solution)/shard_map/while/body/eval_jaxpr/rkgd,ckd->kgrc/dot_general | solution.py:27
  187.0 9.3 %fusion.143 = bf16[2,2,512,1536]{2,3,1,0:T(8,128)(2,1)S(1)} fusion(f32[2,1536,512,2]{2,1,3,0:T(8,128)} %fusion.141, bf16[512,2,2,128]{0,3,2,1:T(8,128)(2,1)} %bitcast.320, f32[2,2,512]{2,1,0:T(2,128)S(1)} %sub.273, f32[2,2,512]{2,1,0:T(2,128)S(1)} %sub.274, pred[512,1536]{0,1:T(8,128)(4,1)S(1)} %fusion.142, ...), kind=kOutput, calls=%fused_computation.2.clone.1 | convolution fusion | flops 824180736 | bytes 20987908 | tf_op jit(solution)/shard_map/while/body/eval_jaxpr/rkgd,ckd->kgrc/dot_general | solution.py:39
  198.2 2.3 fusion.145
  200.4 6.3 %fusion.146 = f32[2560,2,128]{0,2,1:T(8,128)S(1)} fusion(f32[2560,2,128]{0,2,1:T(8,128)S(1)} %copy-done.7, s32[]{:T(128)S(6)} %select_n.114, bf16[512,2,2,128]{0,3,2,1:T(8,128)(2,1)S(1)} %bitcast.321, f32[2,1536,512,2]{2,1,3,0:T(8,128)} %fusion.141, f32[2,2,512]{2,1,0:T(2,128)S(1)} %sub.274, pred[512,1536]{0,1:T(8,128)(4,1)S(1)} %fusion.142), kind=kOutput, calls=%fused_computation.14.clone.1 | convolution fusion | flops 818282496 | bytes 17047556 | tf_op jit(solution)/shard_map/while/body/eval_jaxpr/kgrc,rkgd->ckd/dot_general | solution.py:42
  208.3 2.1 constant_dynamic-slice_fusion.12
  210.4 7.5 %fusion.141 = f32[2,1536,512,2]{2,1,3,0:T(8,128)} fusion(bf16[512,2,2,128]{0,3,2,1:T(8,128)(2,1)S(1)} %bitcast.314, bf16[2560,2,128]{0,2,1:T(8,128)(2,1)} %get-tuple-element.1067, s32[]{:T(128)S(6)} %select_n.114), kind=kOutput, calls=%fused_computation.22.clone.1 | convolution fusion | flops 805306368 | bytes 13893636 | tf_op jit(solution)/shard_map/while/body/eval_jaxpr/rkgd,ckd->kgrc/dot_general | solution.py:27
  219.7 9.3 %fusion.143 = bf16[2,2,512,1536]{2,3,1,0:T(8,128)(2,1)S(1)} fusion(f32[2,1536,512,2]{2,1,3,0:T(8,128)} %fusion.141, bf16[512,2,2,128]{0,3,2,1:T(8,128)(2,1)} %bitcast.320, f32[2,2,512]{2,1,0:T(2,128)S(1)} %sub.273, f32[2,2,512]{2,1,0:T(2,128)S(1)} %sub.274, pred[512,1536]{0,1:T(8,128)(4,1)S(1)} %fusion.142, ...), kind=kOutput, calls=%fused_computation.2.clone.1 | convolution fusion | flops 824180736 | bytes 20987908 | tf_op jit(solution)/shard_map/while/body/eval_jaxpr/rkgd,ckd->kgrc/dot_general | solution.py:39
  230.9 2.3 fusion.145
  233.2 6.3 %fusion.146 = f32[2560,2,128]{0,2,1:T(8,128)S(1)} fusion(f32[2560,2,128]{0,2,1:T(8,128)S(1)} %copy-done.7, s32[]{:T(128)S(6)} %select_n.114, bf16[512,2,2,128]{0,3,2,1:T(8,128)(2,1)S(1)} %bitcast.321, f32[2,1536,512,2]{2,1,3,0:T(8,128)} %fusion.141, f32[2,2,512]{2,1,0:T(2,128)S(1)} %sub.274, pred[512,1536]{0,1:T(8,128)(4,1)S(1)} %fusion.142), kind=kOutput, calls=%fused_computation.14.clone.1 | convolution fusion | flops 818282496 | bytes 17047556 | tf_op jit(solution)/shard_map/while/body/eval_jaxpr/kgrc,rkgd->ckd/dot_general | solution.py:42
  241.0 2.1 constant_dynamic-slice_fusion.12
  243.1 7.5 %fusion.141 = f32[2,1536,512,2]{2,1,3,0:T(8,128)} fusion(bf16[512,2,2,128]{0,3,2,1:T(8,128)(2,1)S(1)} %bitcast.314, bf16[2560,2,128]{0,2,1:T(8,128)(2,1)} %get-tuple-element.1067, s32[]{:T(128)S(6)} %select_n.114), kind=kOutput, calls=%fused_computation.22.clone.1 | convolution fusion | flops 805306368 | bytes 13893636 | tf_op jit(solution)/shard_map/while/body/eval_jaxpr/rkgd,ckd->kgrc/dot_general | solution.py:27
  252.5 9.3 %fusion.143 = bf16[2,2,512,1536]{2,3,1,0:T(8,128)(2,1)S(1)} fusion(f32[2,1536,512,2]{2,1,3,0:T(8,128)} %fusion.141, bf16[512,2,2,128]{0,3,2,1:T(8,128)(2,1)} %bitcast.320, f32[2,2,512]{2,1,0:T(2,128)S(1)} %sub.273, f32[2,2,512]{2,1,0:T(2,128)S(1)} %sub.274, pred[512,1536]{0,1:T(8,128)(4,1)S(1)} %fusion.142, ...), kind=kOutput, calls=%fused_computation.2.clone.1 | convolution fusion | flops 824180736 | bytes 20987908 | tf_op jit(solution)/shard_map/while/body/eval_jaxpr/rkgd,ckd->kgrc/dot_general | solution.py:39
  263.7 2.3 fusion.145
  266.0 6.3 %fusion.146 = f32[2560,2,128]{0,2,1:T(8,128)S(1)} fusion(f32[2560,2,128]{0,2,1:T(8,128)S(1)} %copy-done.7, s32[]{:T(128)S(6)} %select_n.114, bf16[512,2,2,128]{0,3,2,1:T(8,128)(2,1)S(1)} %bitcast.321, f32[2,1536,512,2]{2,1,3,0:T(8,128)} %fusion.141, f32[2,2,512]{2,1,0:T(2,128)S(1)} %sub.274, pred[512,1536]{0,1:T(8,128)(4,1)S(1)} %fusion.142), kind=kOutput, calls=%fused_computation.14.clone.1 | convolution fusion | flops 818282496 | bytes 17047556 | tf_op jit(solution)/shard_map/while/body/eval_jaxpr/kgrc,rkgd->ckd/dot_general | solution.py:42
  273.8 3.8 pad_maximum_fusion
  277.6 8.6 %copy.173 = bf16[2,1536,512]{2,0,1:T(2,128)(2,1)} copy(bf16[2,1536,512]{1,2,0:T(8,128)(2,1)} %pad_maximum_fusion) | data formatting | bytes 6291456 | tf_op jit(solution)/shard_map/stack | solution.py:163
  286.2 5.9 %all-to-all-start = ((bf16[2,1536,512]{2,0,1:T(2,128)(2,1)}), bf16[2,1536,512]{2,0,1:T(2,128)(2,1)}, u32[]{:S(2)}, u32[]{:S(2)}) async-start(bf16[2,1536,512]{2,0,1:T(2,128)(2,1)} %copy.173), calls=%async_computation | async-start | bytes 6291456 | tf_op jit(solution)/shard_map/all_to_all | solution.py:181
  293.8 4.9 %collective-permute-start.2 = (f32[2,1024,2,128]{1,3,2,0:T(8,128)S(1)}, f32[2,1024,2,128]{1,3,2,0:T(8,128)S(1)}, u32[]{:S(2)}, u32[]{:S(2)}) collective-permute-start(f32[2,1024,2,128]{1,3,2,0:T(8,128)S(1)} %pad_maximum_fusion.1), channel_id=1, source_target_pairs={{8,0},{16,8},{24,16},{32,24},{40,32},{48,40},{56,48},{64,56},{72,6... | collective-permute-start | bytes 6291464 | tf_op jit(solution)/shard_map/ppermute | solution.py:16
  302.7 3.2 collective-permute-start.3
  305.9 51.0 %collective-permute-done.2 = f32[2,1024,2,128]{1,3,2,0:T(8,128)S(1)} collective-permute-done((f32[2,1024,2,128]{1,3,2,0:T(8,128)S(1)}, f32[2,1024,2,128]{1,3,2,0:T(8,128)S(1)}, u32[]{:S(2)}, u32[]{:S(2)}) %collective-permute-start.2) | collective-permute-done | bytes 2097184 | tf_op jit(solution)/shard_map/ppermute | solution.py:16
  358.9 5.0 %copy.176 = bf16[2,1536,256]{2,0,1:T(2,128)(2,1)} copy(bf16[2,1536,256]{1,2,0:T(8,128)(2,1)} %pad_maximum_fusion.3) | data formatting | bytes 3145728 | tf_op jit(solution)/shard_map/stack | solution.py:166
  364.0 5.8 %all-to-all-start.1 = ((bf16[2,1536,256]{2,0,1:T(2,128)(2,1)}), bf16[2,1536,256]{2,0,1:T(2,128)(2,1)}, u32[]{:S(2)}, u32[]{:S(2)}) async-start(bf16[2,1536,256]{2,0,1:T(2,128)(2,1)} %copy.176), calls=%async_computation.1 | async-start | bytes 3145728 | tf_op jit(solution)/shard_map/all_to_all | solution.py:182
  369.8 18.2 %collective-permute-done.3 = f32[2,1024,2,128]{1,3,2,0:T(8,128)} collective-permute-done((f32[2,1024,2,128]{1,3,2,0:T(8,128)}, f32[2,1024,2,128]{1,3,2,0:T(8,128)}, u32[]{:S(2)}, u32[]{:S(2)}) %collective-permute-start.3) | collective-permute-done | bytes 2097184 | tf_op jit(solution)/shard_map/ppermute | solution.py:16
  387.9 3.5 fusion.75
  393.2 2.9 copy.179
  397.7 5.4 %all-to-all-start.2 = ((bf16[2,1536,256]{2,0,1:T(2,128)(2,1)}), bf16[2,1536,256]{2,0,1:T(2,128)(2,1)S(1)}, u32[]{:S(2)}, u32[]{:S(2)}) async-start(bf16[2,1536,256]{2,0,1:T(2,128)(2,1)} %copy.179), calls=%async_computation.2 | async-start | bytes 3145728 | tf_op jit(solution)/shard_map/all_to_all | solution.py:183
  403.2 2.4 copy.174
  405.5 2.1 copy.224
  410.6 5.4 %all-to-all-done.2 = bf16[2,1536,256]{2,0,1:T(2,128)(2,1)S(1)} async-done(((bf16[2,1536,256]{2,0,1:T(2,128)(2,1)}), bf16[2,1536,256]{2,0,1:T(2,128)(2,1)S(1)}, u32[]{:S(2)}, u32[]{:S(2)}) %all-to-all-start.2) | async-done | bytes 1572896 | tf_op jit(solution)/shard_map/all_to_all | solution.py:183
  (168 shorter events, 69.2 us)
Async XLA Ops:
  0.6 1.2 slice-start
  1.9 8.9 %copy-start.12 = (bf16[2,1536,256]{2,1,0:T(8,128)(2,1)S(1)}, bf16[2,1536,256]{2,1,0:T(8,128)(2,1)}, u32[]{:S(2)}) copy-start(bf16[2,1536,256]{2,1,0:T(8,128)(2,1)} %param.20) | copy-start | bytes 4718596
  3.2 2.1 slice-start.1
  3.2 57.3 %collective-permute-start = (bf16[2,1024,256]{1,2,0:T(8,128)(2,1)}, bf16[2,1024,256]{1,2,0:T(8,128)(2,1)}, u32[]{:S(2)}, u32[]{:S(2)}) collective-permute-start(bf16[2,1024,256]{1,2,0:T(8,128)(2,1)} %copy.214), channel_id=1, source_target_pairs={{0,8},{8,16},{16,24},{24,32},{32,40},{40,48},{48,56},{56,64},{64,7... | collective-permute-start | bytes 3145736 | tf_op jit(solution)/shard_map/ppermute | solution.py:16
  6.6 5.5 %copy-start.13 = (bf16[2,1536,256]{2,1,0:T(8,128)(2,1)S(1)}, bf16[2,1536,256]{2,1,0:T(8,128)(2,1)}, u32[]{:S(2)}) copy-start(bf16[2,1536,256]{2,1,0:T(8,128)(2,1)} %param.21) | copy-start | bytes 4718596
  6.6 6.7 %copy-start.16 = (bf16[2,1536,512]{2,1,0:T(8,128)(2,1)S(1)}, bf16[2,1536,512]{2,1,0:T(8,128)(2,1)}, u32[]{:S(2)}) copy-start(bf16[2,1536,512]{2,1,0:T(8,128)(2,1)} %param.19) | copy-start | bytes 9437188
  6.6 56.0 %collective-permute-start.1 = (bf16[2,1024,256]{1,2,0:T(8,128)(2,1)}, bf16[2,1024,256]{1,2,0:T(8,128)(2,1)}, u32[]{:S(2)}, u32[]{:S(2)}) collective-permute-start(bf16[2,1024,256]{1,2,0:T(8,128)(2,1)} %copy.217), channel_id=1, source_target_pairs={{0,8},{8,16},{16,24},{24,32},{32,40},{40,48},{48,56},{56,64},{64,7... | collective-permute-start | bytes 3145736 | tf_op jit(solution)/shard_map/ppermute | solution.py:16
  13.4 2.5 copy-start.6
  15.8 2.5 copy-start.17
  56.8 3.1 copy-start.19
  56.8 3.7 copy-start.18
  58.3 6.4 %copy-start.14 = (bf16[1,1536,256]{1,2,0:T(8,128)(2,1)S(1)}, bf16[1,1536,256]{1,2,0:T(8,128)(2,1)}, u32[]{:S(2)}) copy-start(bf16[1,1536,256]{1,2,0:T(8,128)(2,1)} %copy.220) | copy-start | bytes 2359300
  58.3 6.4 %copy-start.15 = (bf16[1,1536,256]{1,2,0:T(8,128)(2,1)S(1)}, bf16[1,1536,256]{1,2,0:T(8,128)(2,1)}, u32[]{:S(2)}) copy-start(bf16[1,1536,256]{1,2,0:T(8,128)(2,1)} %copy.222) | copy-start | bytes 2359300
  81.1 9.3 %copy-start.3 = (bf16[2560,2,128]{0,2,1:T(8,128)(2,1)S(1)}, bf16[2560,2,128]{0,2,1:T(8,128)(2,1)}, u32[]{:S(2)}) copy-start(bf16[2560,2,128]{0,2,1:T(8,128)(2,1)} %get-tuple-element.1013) | copy-start | bytes 3932164 | tf_op jit(solution)/shard_map/while
  92.3 2.3 copy-start.4
  92.3 2.3 copy-start.10
  100.9 1.5 copy-start.11
  113.8 9.3 %copy-start.3 = (bf16[2560,2,128]{0,2,1:T(8,128)(2,1)S(1)}, bf16[2560,2,128]{0,2,1:T(8,128)(2,1)}, u32[]{:S(2)}) copy-start(bf16[2560,2,128]{0,2,1:T(8,128)(2,1)} %get-tuple-element.1013) | copy-start | bytes 3932164 | tf_op jit(solution)/shard_map/while
  125.0 2.3 copy-start.4
  125.0 2.3 copy-start.10
  133.6 1.5 copy-start.11
  146.5 9.3 %copy-start.3 = (bf16[2560,2,128]{0,2,1:T(8,128)(2,1)S(1)}, bf16[2560,2,128]{0,2,1:T(8,128)(2,1)}, u32[]{:S(2)}) copy-start(bf16[2560,2,128]{0,2,1:T(8,128)(2,1)} %get-tuple-element.1013) | copy-start | bytes 3932164 | tf_op jit(solution)/shard_map/while
  157.7 2.3 copy-start.4
  157.7 2.3 copy-start.10
  166.2 1.5 copy-start.11
  167.7 4.4 %copy-start = (f32[2560,2,128]{0,2,1:T(8,128)}, f32[2560,2,128]{0,2,1:T(8,128)S(1)}, u32[]{:S(2)}) copy-start(f32[2560,2,128]{0,2,1:T(8,128)S(1)} %get-tuple-element.630) | copy-start | bytes 7864324
  187.0 9.3 %copy-start.2 = (bf16[2560,2,128]{0,2,1:T(8,128)(2,1)S(1)}, bf16[2560,2,128]{0,2,1:T(8,128)(2,1)}, u32[]{:S(2)}) copy-start(bf16[2560,2,128]{0,2,1:T(8,128)(2,1)} %get-tuple-element.1067) | copy-start | bytes 3932164 | tf_op jit(solution)/shard_map/while
  198.1 2.3 copy-start.5
  198.1 2.3 copy-start.7
  206.7 1.5 copy-start.8
  219.7 9.3 %copy-start.2 = (bf16[2560,2,128]{0,2,1:T(8,128)(2,1)S(1)}, bf16[2560,2,128]{0,2,1:T(8,128)(2,1)}, u32[]{:S(2)}) copy-start(bf16[2560,2,128]{0,2,1:T(8,128)(2,1)} %get-tuple-element.1067) | copy-start | bytes 3932164 | tf_op jit(solution)/shard_map/while
  230.9 2.3 copy-start.5
  230.9 2.3 copy-start.7
  239.5 1.5 copy-start.8
  252.5 9.3 %copy-start.2 = (bf16[2560,2,128]{0,2,1:T(8,128)(2,1)S(1)}, bf16[2560,2,128]{0,2,1:T(8,128)(2,1)}, u32[]{:S(2)}) copy-start(bf16[2560,2,128]{0,2,1:T(8,128)(2,1)} %get-tuple-element.1067) | copy-start | bytes 3932164 | tf_op jit(solution)/shard_map/while
  263.7 2.3 copy-start.5
  263.7 2.3 copy-start.7
  272.2 1.5 copy-start.8
  286.2 77.7 %all-to-all-start = ((bf16[2,1536,512]{2,0,1:T(2,128)(2,1)}), bf16[2,1536,512]{2,0,1:T(2,128)(2,1)}, u32[]{:S(2)}, u32[]{:S(2)}) async-start(bf16[2,1536,512]{2,0,1:T(2,128)(2,1)} %copy.173), calls=%async_computation | async-start | bytes 6291456 | tf_op jit(solution)/shard_map/all_to_all | solution.py:181
  293.8 63.1 %collective-permute-start.2 = (f32[2,1024,2,128]{1,3,2,0:T(8,128)S(1)}, f32[2,1024,2,128]{1,3,2,0:T(8,128)S(1)}, u32[]{:S(2)}, u32[]{:S(2)}) collective-permute-start(f32[2,1024,2,128]{1,3,2,0:T(8,128)S(1)} %pad_maximum_fusion.1), channel_id=1, source_target_pairs={{8,0},{16,8},{24,16},{32,24},{40,32},{48,40},{56,48},{64,56},{72,6... | collective-permute-start | bytes 6291464 | tf_op jit(solution)/shard_map/ppermute | solution.py:16
  301.3 55.7 %copy-start.1 = (f32[2560,2,128]{0,2,1:T(8,128)S(1)}, f32[2560,2,128]{0,2,1:T(8,128)}, u32[]{:S(2)}) copy-start(f32[2560,2,128]{0,2,1:T(8,128)} %copy-done) | copy-start | bytes 7864324
  302.7 85.2 %collective-permute-start.3 = (f32[2,1024,2,128]{1,3,2,0:T(8,128)}, f32[2,1024,2,128]{1,3,2,0:T(8,128)}, u32[]{:S(2)}, u32[]{:S(2)}) collective-permute-start(f32[2,1024,2,128]{1,3,2,0:T(8,128)} %pad_maximum_fusion.2), channel_id=1, source_target_pairs={{8,0},{16,8},{24,16},{32,24},{40,32},{48,40},{56,48},{64,56},{72,6... | collective-permute-start | bytes 6291464 | tf_op jit(solution)/shard_map/ppermute | solution.py:16
  358.9 29.0 %copy-start.9 = (f32[2560,2,128]{0,2,1:T(8,128)S(1)}, f32[2560,2,128]{0,2,1:T(8,128)}, u32[]{:S(2)}) copy-start(f32[2560,2,128]{0,2,1:T(8,128)} %get-tuple-element.631) | copy-start | bytes 7864324
  364.0 33.7 %all-to-all-start.1 = ((bf16[2,1536,256]{2,0,1:T(2,128)(2,1)}), bf16[2,1536,256]{2,0,1:T(2,128)(2,1)}, u32[]{:S(2)}, u32[]{:S(2)}) async-start(bf16[2,1536,256]{2,0,1:T(2,128)(2,1)} %copy.176), calls=%async_computation.1 | async-start | bytes 3145728 | tf_op jit(solution)/shard_map/all_to_all | solution.py:182
  397.7 18.3 %all-to-all-start.2 = ((bf16[2,1536,256]{2,0,1:T(2,128)(2,1)}), bf16[2,1536,256]{2,0,1:T(2,128)(2,1)S(1)}, u32[]{:S(2)}, u32[]{:S(2)}) async-start(bf16[2,1536,256]{2,0,1:T(2,128)(2,1)} %copy.179), calls=%async_computation.2 | async-start | bytes 3145728 | tf_op jit(solution)/shard_map/all_to_all | solution.py:183
where the time goes:
time: 420 us; the launch traced here: 418 us
  matrix products  158 us (38%)
  local copies, waits for them, and re-layouts  112 us (27%)
  waiting for transfers between devices  76.3 us (18%)
  other arithmetic  38.5 us (9%)
  starting transfers between devices  31.4 us (7%)
    ppermute x4, waiting for transfers between devices, shifted(): lax.ppermute(value, axis, [(source, source + steps) for source in range(f...  69.2 us
    dot_general x6, matrix products, block_grads(): jnp.einsum('rkgd,ckd->kgrc', do_heads, v_block, preferred_element_type=jn...  55.9 us
    dot_general x6, matrix products, block_grads(): jnp.einsum('rkgd,ckd->kgrc', query_head_count, k_block, preferred_element...  45 us
    dot_general x6, matrix products, block_grads(): jnp.einsum('kgrc,rkgd->ckd', prob_low, do_heads, preferred_element_type=j...  37.6 us
    unnamed x34, local copies, waits for them, and re-layouts  22.5 us
    ppermute x4, starting transfers between devices, shifted(): lax.ppermute(value, axis, [(source, source + steps) for source in range(f...  14.3 us
    dot_general x6, matrix products, block_grads(): jnp.einsum('kgrc,rkgd->ckd', score_low, query_head_count, preferred_eleme...  13.6 us
    dynamic_slice x6, local copies, waits for them, and re-layouts, step(): do_block = lax.dynamic_slice_in_dim(do_all, start_row, BLOCK, 0)  12.6 us
  transfers between devices with their start and end apart: 7, of which 4 were waited for; matrix products, arithmetic and copies ran while one was open for 19% of the time, Pallas kernels for 0%

commit v1 on v0

v1 whole, which is shorter than its diff:
```python
import functools
import math

import jax
import jax.numpy as jnp
from jax import lax
from jax.experimental import pallas as pl
from jax.experimental.pallas import tpu as pltpu
from jax.sharding import PartitionSpec as P

HEAD_SIZE = 128
WINDOW_LENGTH = 1024
QUERY_PRE = 168
SLIDING_LAYERS = 2
ROWS = 128
SCALE = QUERY_PRE ** (-0.5)
LOG2_E = math.log2(math.e)
HIDDEN = -1e30
MESH = pl.DeviceIdType.MESH
BIASED = (0, 4, 5, 6, 7, 8)
NT = (((1,), (1,)), ((), ()))
NN = (((1,), (0,)), ((), ()))


def dot(a, b, dims=NN):
    return lax.dot_general(a, b, dims, preferred_element_type=jnp.float32)


def kernel(
    head_count,
    ctx_count,
    win_ref,
    lse_ref,
    q_hbm,
    k_hbm,
    v_hbm,
    o_hbm,
    g_hbm,
    dq_out,
    dk_out,
    dv_out,
    q_all,
    g_all,
    o_all,
    k_ext,
    v_ext,
    k_turned,
    bias,
    prob_buf,
    score_buf,
    dk_acc,
    dv_acc,
    dq_stage,
    dk_stage,
    dv_stage,
    back_send,
    back_recv,
    load_sem,
    rim_send_sem,
    rim_recv_sem,
    back_send_sem,
    back_recv_sem,
    out_send_sem,
    out_recv_sem,
    own_sem,
):
    ctx = lax.axis_index("ctx")
    head = lax.axis_index("head")
    tokens = q_hbm.shape[1]
    groups = k_hbm.shape[2] // HEAD_SIZE
    units = SLIDING_LAYERS * groups
    ext = WINDOW_LENGTH + tokens
    chunk = tokens // head_count
    halo_blocks = WINDOW_LENGTH // ROWS
    blocks = tokens // ROWS
    span = WINDOW_LENGTH + ROWS
    pair = 2 * HEAD_SIZE
    after = lax.rem(ctx + 1, ctx_count)
    before = lax.rem(ctx + ctx_count - 1, ctx_count)
    has_before = ctx > 0
    has_after = ctx < ctx_count - 1

    def place(unit):
        return unit // groups, lax.rem(unit, groups)

    def loads(unit):
        layer, group = place(unit)
        wide = pl.ds(pl.multiple_of(group * pair, pair), pair)
        slim = pl.ds(pl.multiple_of(group * HEAD_SIZE, HEAD_SIZE), HEAD_SIZE)
        return [
            pltpu.make_async_copy(
                k_hbm.at[layer, :, slim], k_ext.at[unit, pl.ds(WINDOW_LENGTH, tokens)], load_sem.at[0, unit]
            ),
            pltpu.make_async_copy(
                v_hbm.at[layer, :, slim], v_ext.at[unit, pl.ds(WINDOW_LENGTH, tokens)], load_sem.at[1, unit]
            ),
            pltpu.make_async_copy(q_hbm.at[layer, :, wide], q_all.at[unit], load_sem.at[2, unit]),
            pltpu.make_async_copy(g_hbm.at[layer, :, wide], g_all.at[unit], load_sem.at[3, unit]),
            pltpu.make_async_copy(o_hbm.at[layer, :, wide], o_all.at[unit], load_sem.at[4, unit]),
        ]

    def rims(unit):
        layer, group = place(unit)
        slim = pl.ds(pl.multiple_of(group * HEAD_SIZE, HEAD_SIZE), HEAD_SIZE)
        last = pl.ds(tokens - WINDOW_LENGTH, WINDOW_LENGTH)
        first = pl.ds(0, WINDOW_LENGTH)
        return [
            pltpu.make_async_remote_copy(
                src_ref=source.at[layer, last, slim],
                dst_ref=target.at[unit, first],
                send_sem=rim_send_sem.at[which, unit],
                recv_sem=rim_recv_sem.at[which, unit],
                device_id=(after, head),
                device_id_type=MESH,
            )
            for which, (source, target) in enumerate(((k_hbm, k_ext), (v_hbm, v_ext)))
        ]

    def backs(unit):
        return [
            pltpu.make_async_remote_copy(
                src_ref=back_send.at[which, unit],
                dst_ref=back_recv.at[which, unit],
                send_sem=back_send_sem.at[which, unit],
                recv_sem=back_recv_sem.at[which, unit],
                device_id=(before, head),
                device_id_type=MESH,
            )
            for which in range(2)
        ]

    def exchange(unit, step, which):
        layer, group = place(unit)
        stage, target, width = (
            (dq_stage, dq_out, pair),
            (dk_stage, dk_out, HEAD_SIZE),
            (dv_stage, dv_out, HEAD_SIZE),
        )[which]
        other = lax.rem(head + step, head_count)
        rows = pl.ds(pl.multiple_of(other * chunk, chunk), chunk)
        columns = pl.ds(pl.multiple_of((head * groups + group) * width, width), width)
        if step == 0:
            return pltpu.make_async_copy(
                stage.at[unit, rows], target.at[layer, :, columns], own_sem.at[which, unit]
            )
        return pltpu.make_async_remote_copy(
            src_ref=stage.at[unit, rows],
            dst_ref=target.at[layer, :, columns],
            send_sem=out_send_sem.at[which, unit, step],
            recv_sem=out_recv_sem.at[which, unit, step],
            device_id=(ctx, other),
            device_id_type=MESH,
        )

    for copy in loads(0):
        copy.start()

    barrier = pltpu.get_barrier_semaphore()
    for step in range(1, head_count):
        pl.semaphore_signal(
            barrier, inc=1, device_id=(ctx, lax.rem(head + step, head_count)), device_id_type=MESH
        )
    for other in (before, after):
        pl.semaphore_signal(barrier, inc=1, device_id=(other, head), device_id_type=MESH)

    down = lax.broadcasted_iota(jnp.int32, (ROWS, ROWS), 0)
    along = lax.broadcasted_iota(jnp.int32, (ROWS, ROWS), 1)
    for layer in range(SLIDING_LAYERS):
        win = win_ref[layer]
        for slot, distance in enumerate(BIASED):
            apart = along - down + ROWS * distance
            seen = (apart >= 0) & (apart < win)
            bias[layer, slot] = jnp.where(seen, 0.0, HIDDEN)

    @pl.when(jnp.logical_not(has_before))
    def _():
        for unit in range(units):
            k_ext[unit, pl.ds(0, WINDOW_LENGTH)] = jnp.zeros((WINDOW_LENGTH, HEAD_SIZE), jnp.bfloat16)
            v_ext[unit, pl.ds(0, WINDOW_LENGTH)] = jnp.zeros((WINDOW_LENGTH, HEAD_SIZE), jnp.bfloat16)

    @pl.when(jnp.logical_not(has_after))
    def _():
        for which in range(2):
            for unit in range(units):
                back_recv[which, unit] = jnp.zeros((WINDOW_LENGTH, HEAD_SIZE), jnp.bfloat16)

    pl.semaphore_wait(barrier, head_count + 1)

    @pl.when(has_after)
    def _():
        for unit in range(units):
            for copy in rims(unit):
                copy.start()

    for unit in range(1, units):
        for copy in loads(unit):
            copy.start()

    def turn(unit, lower, upper):
        def step(index, carry):
            rows = pl.ds(pl.multiple_of(index * ROWS, ROWS), ROWS)
            k_turned[:, rows] = k_ext[unit, rows].astype(jnp.float32).T.astype(jnp.bfloat16)
            return carry

        lax.fori_loop(lower, upper, step, 0)

    def block(unit, index):
        layer, group = place(unit)
        start = pl.multiple_of(index * ROWS, ROWS)
        rows = pl.ds(start, ROWS)

        def stacked(ref):
            both = ref[unit, rows]
            return jnp.concatenate([both[:, :HEAD_SIZE], both[:, HEAD_SIZE:]], 0)

        q_rows = stacked(q_all)
        g_rows = stacked(g_all)
        product = g_rows.astype(jnp.float32) * stacked(o_all).astype(jnp.float32)
        high = product.astype(jnp.bfloat16)
        low = (product - high.astype(jnp.float32)).astype(jnp.bfloat16)
        delta = dot(
            jnp.ones((8, 2 * HEAD_SIZE), jnp.bfloat16), jnp.concatenate([high, low], 1), NT
        )[0:1]
        norms = lse_ref[layer, :, rows]
        lse = jnp.concatenate([norms[0:1], norms[1:2]], 1)
        for other in range(1, groups):
            mine = jnp.concatenate([norms[2 * other : 2 * other + 1], norms[2 * other + 1 : 2 * other + 2]], 1)
            lse = jnp.where(group == other, mine, lse)
        lse = lse * LOG2_E
        pieces = span // ROWS
        per = 3
        for first in range(0, pieces, per):
            keys = pl.ds(pl.multiple_of(start + first * ROWS, ROWS), per * ROWS)
            scores = dot(k_ext[unit, keys], q_rows, NT)
            grad_prob = dot(v_ext[unit, keys], g_rows, NT)
            for n in range(per):
                piece = first + n
                distance = pieces - 1 - piece
                outside = jnp.logical_and(jnp.logical_not(has_before), index + piece < halo_blocks)
                offset = lse + jnp.where(outside, -HIDDEN, 0.0)
                part = slice(n * ROWS, (n + 1) * ROWS)
                power = scores[part] * (SCALE * LOG2_E) - offset
                if distance in BIASED:
                    add = bias[layer, BIASED.index(distance)]
                    power = power + jnp.concatenate([add, add], 1)
                prob = jnp.exp2(power)
                grad_score = prob * (grad_prob[part] - delta)
                target = pl.ds(piece * ROWS, ROWS)
                prob_buf[target] = prob.astype(jnp.bfloat16)
                score_buf[target] = grad_score.astype(jnp.bfloat16)
        window = pl.ds(start, span)
        dv_acc[unit, window] += dot(prob_buf[...], g_rows)
        dk_acc[unit, window] += dot(score_buf[...], q_rows)
        dq = (dot(k_turned[:, window], score_buf[...]) * SCALE).T.astype(jnp.bfloat16)
        dq_stage[unit, rows, pl.ds(0, HEAD_SIZE)] = dq[:ROWS]
        dq_stage[unit, rows, pl.ds(HEAD_SIZE, HEAD_SIZE)] = dq[ROWS:]

    def sweep(unit, lower, upper):
        def step(index, carry):
            block(unit, index)
            return carry

        lax.fori_loop(lower, upper, step, 0)

    def finish(unit):
        @pl.when(has_after)
        def _():
            for copy in backs(unit):
                copy.wait_recv()

        own = tokens - WINDOW_LENGTH
        for which, (acc, stage) in enumerate(((dk_acc, dk_stage), (dv_acc, dv_stage))):
            factor = SCALE if which == 0 else 1.0

            def step(index, carry, acc=acc, stage=stage, which=which, factor=factor):
                rows = pl.ds(pl.multiple_of(index * ROWS, ROWS), ROWS)
                source = pl.ds(pl.multiple_of(index * ROWS + WINDOW_LENGTH + own, ROWS), ROWS)
                total = acc[unit, source] * factor + back_recv[which, unit, rows].astype(jnp.float32)
                stage[unit, pl.ds(pl.multiple_of(index * ROWS + own, ROWS), ROWS)] = total.astype(jnp.bfloat16)
                return carry

            stage[unit, pl.ds(0, own)] = (acc[unit, pl.ds(WINDOW_LENGTH, own)] * factor).astype(jnp.bfloat16)
            lax.fori_loop(0, halo_blocks, step, 0)
        for step in list(range(1, head_count)) + [0]:
            for which in (1, 2):
                exchange(unit, step, which).start()

    def one_unit(unit, carry):
        for copy in loads(unit):
            copy.wait()
        dk_acc[unit] = jnp.zeros((ext, HEAD_SIZE), jnp.float32)
        dv_acc[unit] = jnp.zeros((ext, HEAD_SIZE), jnp.float32)
        turn(unit, halo_blocks, halo_blocks + blocks)
        sweep(unit, halo_blocks, blocks)

        @pl.when(unit > 0)
        def _():
            finish(unit - 1)

        @pl.when(has_before)
        def _():
            for copy in rims(unit):
                copy.wait_recv()

        turn(unit, 0, halo_blocks)
        sweep(unit, 0, halo_blocks)
        for which, (acc, factor) in enumerate(((dk_acc, SCALE), (dv_acc, 1.0))):
            back_send[which, unit] = (acc[unit, pl.ds(0, WINDOW_LENGTH)] * factor).astype(jnp.bfloat16)

        @pl.when(has_before)
        def _():
            for copy in backs(unit):
                copy.start()

        for step in list(range(1, head_count)) + [0]:
            exchange(unit, step, 0).start()
        return carry

    lax.fori_loop(0, units, one_unit, 0)
    finish(units - 1)

    def drain(unit, carry):
        @pl.when(has_after)
        def _():
            for copy in rims(unit):
                copy.wait_send()

        @pl.when(has_before)
        def _():
            for copy in backs(unit):
                copy.wait_send()

        for which in range(3):
            exchange(unit, 0, which).wait()
            for step in range(1, head_count):
                exchange(unit, step, which).wait()
        return carry

    lax.fori_loop(0, units, drain, 0)


def shards(ctx_count, head_count, queries, keys, values, attn_out, grad_out, log_norm, window):
    tokens = queries.shape[1]
    groups = keys.shape[2] // HEAD_SIZE
    units = SLIDING_LAYERS * groups
    ext = WINDOW_LENGTH + tokens
    pair = 2 * HEAD_SIZE
    span = WINDOW_LENGTH + ROWS
    rows_out = tokens // head_count
    low, wide = jnp.bfloat16, jnp.float32
    anywhere = pl.BlockSpec(memory_space=pl.ANY)
    dma = pltpu.SemaphoreType.DMA
    return pl.pallas_call(
        functools.partial(kernel, head_count, ctx_count),
        out_shape=(
            jax.ShapeDtypeStruct((SLIDING_LAYERS, rows_out, queries.shape[2] * head_count), low),
            jax.ShapeDtypeStruct((SLIDING_LAYERS, rows_out, keys.shape[2] * head_count), low),
            jax.ShapeDtypeStruct((SLIDING_LAYERS, rows_out, values.shape[2] * head_count), low),
        ),
        in_specs=[
            pl.BlockSpec(memory_space=pltpu.SMEM),
            pl.BlockSpec(memory_space=pltpu.VMEM),
            anywhere,
            anywhere,
            anywhere,
            anywhere,
            anywhere,
        ],
        out_specs=(anywhere, anywhere, anywhere),
        scratch_shapes=[
            pltpu.VMEM((units, tokens, pair), low),
            pltpu.VMEM((units, tokens, pair), low),
            pltpu.VMEM((units, tokens, pair), low),
            pltpu.VMEM((units, ext, HEAD_SIZE), low),
            pltpu.VMEM((units, ext, HEAD_SIZE), low),
            pltpu.VMEM((HEAD_SIZE, ext), low),
            pltpu.VMEM((SLIDING_LAYERS, len(BIASED), ROWS, ROWS), wide),
            pltpu.VMEM((span, 2 * ROWS), low),
            pltpu.VMEM((span, 2 * ROWS), low),
            pltpu.VMEM((units, ext, HEAD_SIZE), wide),
            pltpu.VMEM((units, ext, HEAD_SIZE), wide),
            pltpu.VMEM((units, tokens, pair), low),
            pltpu.VMEM((units, tokens, HEAD_SIZE), low),
            pltpu.VMEM((units, tokens, HEAD_SIZE), low),
            pltpu.VMEM((2, units, WINDOW_LENGTH, HEAD_SIZE), low),
            pltpu.VMEM((2, units, WINDOW_LENGTH, HEAD_SIZE), low),
            dma((5, units)),
            dma((2, units)),
            dma((2, units)),
            dma((2, units)),
            dma((2, units)),
            dma((3, units, head_count)),
            dma((3, units, head_count)),
            dma((3, units)),
        ],
        compiler_params=pltpu.CompilerParams(
            collective_id=0, has_side_effects=True, vmem_limit_bytes=60 * 2**20
        ),
        name="band_grads",
    )(window, log_norm, queries, keys, values, attn_out, grad_out)


def solution(mesh):
    in_specs = (
        P(None, "ctx", "head"),
        P(None, "ctx", "head"),
        P(None, "ctx", "head"),
        P(None, "ctx", "head"),
        P(None, "ctx", "head"),
        P(None, "head", "ctx"),
        P(),
    )
    out_specs = (
        P(None, ("ctx", "head"), None),
        P(None, ("ctx", "head"), None),
        P(None, ("ctx", "head"), None),
    )
    body = functools.partial(shards, mesh.shape["ctx"], mesh.shape["head"])
    return jax.shard_map(body, mesh=mesh, in_specs=in_specs, out_specs=out_specs, check_vma=False)
```

time: 420 us -> 124 us (0.30)
  matrix products: 158 us -> 0 us
  Pallas kernels: 0 us -> 114 us
  local copies, waits for them, and re-layouts: 112 us -> 7.15 us
  waiting for transfers between devices: 76.3 us -> 0 us
  other arithmetic: 38.5 us -> 0 us
  starting transfers between devices: 31.4 us -> 0 us
    dot_general x30 -> x0, matrix products: 158 us -> none  [the longest x6 55.9 us: block_grads(): jnp.einsum('rkgd,ckd->kgrc', do_heads, v_block, preferred_element_type=jn...]
    pallas_call x0 -> x1, Pallas kernels: none -> 114 us  [shards(): pl.pallas_call(functools.partial(kernel, head_count, ctx_count), out_shap...]
    ppermute x4 -> x0, waiting for transfers between devices: 69.2 us -> none  [shifted(): lax.ppermute(value, axis, [(source, source + steps) for source in range(f...]
    another operation x13 -> x0, local copies, waits for them, and re-layouts: 27.2 us -> none  [the longest x1 8.63 us: shards(): jnp.stack([entry[0].reshape(tok_local, head_local * HEAD_SIZE) for entry...]
    all_to_all x3 -> x0, starting transfers between devices: 17.1 us -> none  [the longest x1 5.92 us: shards(): lax.all_to_all(dq_stack, 'head', split_axis=1, concat_axis=2, tiled=True)]
    unnamed x34 -> x7, local copies, waits for them, and re-layouts: 22.5 us -> 7.15 us
    ppermute x4 -> x0, starting transfers between devices: 14.3 us -> none  [shifted(): lax.ppermute(value, axis, [(source, source + steps) for source in range(f...]
    slice x15 -> x0, local copies, waits for them, and re-layouts: 13.1 us -> none  [the longest x1 2.13 us: shards(): rim_values[layer_number]]
  transfers between devices with their start and end apart: 7 -> 0, of which waited for: 4 -> 0; matrix products, arithmetic and copies ran while one was open for 19% -> 0% of each run, Pallas kernels for 0% -> 0%
where the time goes in v1:
time: 124 us; the launch traced here: 122 us
  Pallas kernels  114 us (92%)
  local copies, waits for them, and re-layouts  7.15 us (6%)
    pallas_call x1, Pallas kernels, shards(): pl.pallas_call(functools.partial(kernel, head_count, ctx_count), out_shap...  114 us
    unnamed x7, local copies, waits for them, and re-layouts  7.15 us

profile of v1, /device:TPU:6, one launch (start us, length us, event | category | flops | bytes accessed | tf_op | source)
XLA Modules:
  0.0 121.6 jit_solution(8318976669206420323)
XLA Ops:
  0.6 113.8 %band_grads.1 = (bf16[2,192,4096]{2,1,0:T(8,128)(2,1)}, bf16[2,192,2048]{2,1,0:T(8,128)(2,1)}, bf16[2,192,2048]{2,1,0:T(8,128)(2,1)}) custom-call(s32[2]{0:T(128)} %win_ref.1, f32[2,4,1536]{2,1,0:T(4,128)} %lse_ref.1, bf16[2,1536,512]{2,1,0:T(8,128)(2,1)} %q_hbm.1, bf16[2,1536,256]{2,1,0:T(8,128)(2,1)} %k_hbm.1, bf16[2,1536,256]{2,1,0:T(8,128)(2,1)} %v_hbm.1, ...), custom_call_target="tpu_custom_call" | custom-call | tf_op jit(solution)/shard_map/band_grads/pallas_call | solution.py:353
  114.5 0.0 copy-start.1
  114.5 4.0 %copy.13 = bf16[2,192,4096]{2,1,0:T(8,128)(2,1)} copy(bf16[2,192,4096]{2,1,0:T(8,128)(2,1)} %get-tuple-element.6) | data formatting | bytes 6291456
  118.5 0.0 copy-done.1
  118.5 0.0 copy-start
  118.5 1.1 copy.14
  119.7 0.8 copy-done
  120.5 1.1 copy.15
Async XLA Ops:
  114.5 4.0 %copy-start.1 = (bf16[2,192,2048]{2,1,0:T(8,128)(2,1)S(1)}, bf16[2,192,2048]{2,1,0:T(8,128)(2,1)}, u32[]{:S(2)}) copy-start(bf16[2,192,2048]{2,1,0:T(8,128)(2,1)} %get-tuple-element.7) | copy-start | bytes 4718596
  118.5 2.0 %copy-start = (bf16[2,192,2048]{2,1,0:T(8,128)(2,1)S(1)}, bf16[2,192,2048]{2,1,0:T(8,128)(2,1)}, u32[]{:S(2)}) copy-start(bf16[2,192,2048]{2,1,0:T(8,128)(2,1)} %get-tuple-element.8) | copy-start | bytes 4718596

commit v2 on v1

--- a/solution.py
+++ b/solution.py
@@ -17,6 +17,7 @@
 LOG2_E = math.log2(math.e)
 HIDDEN = -1e30
 MESH = pl.DeviceIdType.MESH
+ORDER = ((1, 2), (0, 2), (1, 1), (0, 3), (1, 3), (0, 1), (1, 0))
 BIASED = (0, 4, 5, 6, 7, 8)
 NT = (((1,), (1,)), ((), ()))
 NN = (((1,), (0,)), ((), ()))
@@ -55,6 +56,7 @@
     dv_stage,
     back_send,
     back_recv,
+    relay,
     load_sem,
     rim_send_sem,
     rim_recv_sem,
@@ -63,6 +65,8 @@
     out_send_sem,
     out_recv_sem,
     own_sem,
+    relay_send_sem,
+    relay_recv_sem,
 ):
     ctx = lax.axis_index("ctx")
     head = lax.axis_index("head")
@@ -79,6 +83,15 @@
     before = lax.rem(ctx + ctx_count - 1, ctx_count)
     has_before = ctx > 0
     has_after = ctx < ctx_count - 1
+    seam = ctx_count // 2
+    at_seam = (ctx == seam - 1) | (ctx == seam)
+    passes_rim = (ctx < seam - 2) & (lax.rem(ctx, 2) == 1)
+    passes_back = (ctx >= seam + 2) & (lax.rem(ctx, 2) == 0)
+    rim_unit = (ctx + 1) // 2
+    back_unit = (ctx - seam - 2) // 2
+    last_unit = units - 1
+    to_seam = ctx - (seam - 1)
+    lag = 1 - (to_seam * to_seam + ctx_count * ctx_count - 1) // (ctx_count * ctx_count)
 
     def place(unit):
         return unit // groups, lax.rem(unit, groups)
@@ -99,7 +112,17 @@
             pltpu.make_async_copy(o_hbm.at[layer, :, wide], o_all.at[unit], load_sem.at[4, unit]),
         ]
 
-    def rims(unit):
+    def relay_in(which):
+        return pltpu.make_async_remote_copy(
+            src_ref=relay.at[which],
+            dst_ref=relay.at[which],
+            send_sem=relay_send_sem.at[which],
+            recv_sem=relay_recv_sem.at[which],
+            device_id=(seam, head),
+            device_id_type=MESH,
+        )
+
+    def rims(unit, relayed=False):
         layer, group = place(unit)
         slim = pl.ds(pl.multiple_of(group * HEAD_SIZE, HEAD_SIZE), HEAD_SIZE)
         last = pl.ds(tokens - WINDOW_LENGTH, WINDOW_LENGTH)
@@ -107,47 +130,87 @@
         return [
             pltpu.make_async_remote_copy(
                 src_ref=source.at[layer, last, slim],
-                dst_ref=target.at[unit, first],
+                dst_ref=relay.at[which] if relayed else target.at[unit, first],
                 send_sem=rim_send_sem.at[which, unit],
-                recv_sem=rim_recv_sem.at[which, unit],
-                device_id=(after, head),
+                recv_sem=relay_recv_sem.at[which] if relayed else rim_recv_sem.at[which, unit],
+                device_id=(2 * unit - 1 if relayed else after, head),
                 device_id_type=MESH,
             )
             for which, (source, target) in enumerate(((k_hbm, k_ext), (v_hbm, v_ext)))
         ]
 
-    def backs(unit):
+    def rims_onward():
         return [
             pltpu.make_async_remote_copy(
-                src_ref=back_send.at[which, unit],
-                dst_ref=back_recv.at[which, unit],
-                send_sem=back_send_sem.at[which, unit],
-                recv_sem=back_recv_sem.at[which, unit],
-                device_id=(before, head),
+                src_ref=relay.at[which],
+                dst_ref=target.at[rim_unit, pl.ds(0, WINDOW_LENGTH)],
+                send_sem=relay_send_sem.at[which],
+                recv_sem=rim_recv_sem.at[which, rim_unit],
+                device_id=(seam, head),
+                device_id_type=MESH,
+            )
+            for which, target in enumerate((k_ext, v_ext))
+        ]
+
+    def backs_onward():
+        return [
+            pltpu.make_async_remote_copy(
+                src_ref=relay.at[which],
+                dst_ref=back_recv.at[which, back_unit],
+                send_sem=relay_send_sem.at[which],
+                recv_sem=back_recv_sem.at[which, back_unit],
+                device_id=(seam - 1, head),
                 device_id_type=MESH,
             )
             for which in range(2)
         ]
 
-    def exchange(unit, step, which):
+    def backs(unit, relayed=False):
+        return [
+            pltpu.make_async_remote_copy(
+                src_ref=back_send.at[which, unit],
+                dst_ref=relay.at[which] if relayed else back_recv.at[which, unit],
+                send_sem=back_send_sem.at[which, unit],
+                recv_sem=relay_recv_sem.at[which] if relayed else back_recv_sem.at[which, unit],
+                device_id=(seam + 2 + 2 * unit if relayed else before, head),
+                device_id_type=MESH,
+            )
+            for which in range(2)
+        ]
+
+    def piece_of(unit, other, which):
         layer, group = place(unit)
         stage, target, width = (
             (dq_stage, dq_out, pair),
             (dk_stage, dk_out, HEAD_SIZE),
             (dv_stage, dv_out, HEAD_SIZE),
         )[which]
-        other = lax.rem(head + step, head_count)
         rows = pl.ds(pl.multiple_of(other * chunk, chunk), chunk)
         columns = pl.ds(pl.multiple_of((head * groups + group) * width, width), width)
-        if step == 0:
-            return pltpu.make_async_copy(
-                stage.at[unit, rows], target.at[layer, :, columns], own_sem.at[which, unit]
-            )
+        return stage.at[unit, rows], target.at[layer, :, columns]
+
+    def keep(unit, which):
+        source, target = piece_of(unit, head, which)
+        return pltpu.make_async_copy(source, target, own_sem.at[which, unit])
+
+    def give(unit, other, which):
+        source, target = piece_of(unit, other, which)
         return pltpu.make_async_remote_copy(
-            src_ref=stage.at[unit, rows],
-            dst_ref=target.at[layer, :, columns],
-            send_sem=out_send_sem.at[which, unit, step],
-            recv_sem=out_recv_sem.at[which, unit, step],
+            src_ref=source,
+            dst_ref=target,
+            send_sem=out_send_sem.at[which, unit, other],
+            recv_sem=out_recv_sem.at[which, unit, head],
+            device_id=(ctx, other),
+            device_id_type=MESH,
+        )
+
+    def taken(unit, other, which):
+        source, target = piece_of(unit, other, which)
+        return pltpu.make_async_remote_copy(
+            src_ref=source,
+            dst_ref=target,
+            send_sem=out_send_sem.at[which, unit, other],
+            recv_sem=out_recv_sem.at[which, unit, other],
             device_id=(ctx, other),
             device_id_type=MESH,
         )
@@ -162,6 +225,18 @@
         )
     for other in (before, after):
         pl.semaphore_signal(barrier, inc=1, device_id=(other, head), device_id_type=MESH)
+
+    relays = [2 * unit - 1 for unit in range(1, units)] + [seam + 2 + 2 * unit for unit in range(last_unit)]
+
+    @pl.when(at_seam)
+    def _():
+        for other in relays:
+            pl.semaphore_signal(barrier, inc=1, device_id=(other, head), device_id_type=MESH)
+
+    @pl.when(passes_rim | passes_back)
+    def _():
+        for other in (seam - 1, seam):
+            pl.semaphore_signal(barrier, inc=1, device_id=(other, head), device_id_type=MESH)
 
     down = lax.broadcasted_iota(jnp.int32, (ROWS, ROWS), 0)
     along = lax.broadcasted_iota(jnp.int32, (ROWS, ROWS), 1)
@@ -184,12 +259,30 @@
             for unit in range(units):
                 back_recv[which, unit] = jnp.zeros((WINDOW_LENGTH, HEAD_SIZE), jnp.bfloat16)
 
-    pl.semaphore_wait(barrier, head_count + 1)
-
-    @pl.when(has_after)
+    passes = passes_rim | passes_back
+
+    @pl.when(at_seam)
+    def _():
+        pl.semaphore_wait(barrier, head_count + 1 + len(relays))
+
+    @pl.when(passes)
+    def _():
+        pl.semaphore_wait(barrier, head_count + 3)
+
+    @pl.when(jnp.logical_not(at_seam | passes))
+    def _():
+        pl.semaphore_wait(barrier, head_count + 1)
+
+    @pl.when(has_after & (ctx != seam - 1))
     def _():
         for unit in range(units):
             for copy in rims(unit):
+                copy.start()
+
+    @pl.when(ctx == seam - 1)
+    def _():
+        for unit in range(units):
+            for copy in rims(unit, relayed=unit > 0):
                 copy.start()
 
     for unit in range(1, units):
@@ -204,7 +297,7 @@
 
         lax.fori_loop(lower, upper, step, 0)
 
-    def block(unit, index):
+    def block(unit, index, slot):
         layer, group = place(unit)
         start = pl.multiple_of(index * ROWS, ROWS)
         rows = pl.ds(start, ROWS)
@@ -246,21 +339,18 @@
                 prob = jnp.exp2(power)
                 grad_score = prob * (grad_prob[part] - delta)
                 target = pl.ds(piece * ROWS, ROWS)
-                prob_buf[target] = prob.astype(jnp.bfloat16)
-                score_buf[target] = grad_score.astype(jnp.bfloat16)
+                prob_buf[slot, target] = prob.astype(jnp.bfloat16)
+                score_buf[slot, target] = grad_score.astype(jnp.bfloat16)
         window = pl.ds(start, span)
-        dv_acc[unit, window] += dot(prob_buf[...], g_rows)
-        dk_acc[unit, window] += dot(score_buf[...], q_rows)
-        dq = (dot(k_turned[:, window], score_buf[...]) * SCALE).T.astype(jnp.bfloat16)
+        dv_acc[unit, window] += dot(prob_buf[slot], g_rows)
+        dk_acc[unit, window] += dot(score_buf[slot], q_rows)
+        dq = (dot(k_turned[:, window], score_buf[slot]) * SCALE).T.astype(jnp.bfloat16)
         dq_stage[unit, rows, pl.ds(0, HEAD_SIZE)] = dq[:ROWS]
         dq_stage[unit, rows, pl.ds(HEAD_SIZE, HEAD_SIZE)] = dq[ROWS:]
 
-    def sweep(unit, lower, upper):
-        def step(index, carry):
-            block(unit, index)
-            return carry
-
-        lax.fori_loop(lower, upper, step, 0)
+    def moved_head(across, along):
+        line = head_count // 2
+        return lax.rem(head // line + across, 2) * line + lax.rem(lax.rem(head, line) + along, line)
 
     def finish(unit):
         @pl.when(has_after)
@@ -281,9 +371,11 @@
 
             stage[unit, pl.ds(0, own)] = (acc[unit, pl.ds(WINDOW_LENGTH, own)] * factor).astype(jnp.bfloat16)
             lax.fori_loop(0, halo_blocks, step, 0)
-        for step in list(range(1, head_count)) + [0]:
+        for across, along in ORDER:
             for which in (1, 2):
-                exchange(unit, step, which).start()
+                give(unit, moved_head(across, along), which).start()
+        for which in (1, 2):
+            keep(unit, which).start()
 
     def one_unit(unit, carry):
         for copy in loads(unit):
@@ -291,33 +383,82 @@
         dk_acc[unit] = jnp.zeros((ext, HEAD_SIZE), jnp.float32)
         dv_acc[unit] = jnp.zeros((ext, HEAD_SIZE), jnp.float32)
         turn(unit, halo_blocks, halo_blocks + blocks)
-        sweep(unit, halo_blocks, blocks)
-
-        @pl.when(unit > 0)
-        def _():
-            finish(unit - 1)
-
-        @pl.when(has_before)
-        def _():
-            for copy in rims(unit):
-                copy.wait_recv()
-
-        turn(unit, 0, halo_blocks)
-        sweep(unit, 0, halo_blocks)
-        for which, (acc, factor) in enumerate(((dk_acc, SCALE), (dv_acc, 1.0))):
-            back_send[which, unit] = (acc[unit, pl.ds(0, WINDOW_LENGTH)] * factor).astype(jnp.bfloat16)
-
-        @pl.when(has_before)
-        def _():
-            for copy in backs(unit):
-                copy.start()
-
-        for step in list(range(1, head_count)) + [0]:
-            exchange(unit, step, 0).start()
+        later = (unit + units - 1) // units
+
+        def one_group(step, carry):
+            apart = step - 3 * later
+            moved = (apart * apart + 8) // 9
+            group = 3 * (1 - moved) + moved * lax.rem(head + step, 3)
+
+            @pl.when(step == 1 - later)
+            def _():
+                @pl.when(has_before)
+                def _():
+                    for copy in rims(unit):
+                        copy.wait_recv()
+
+                turn(unit, 0, halo_blocks)
+
+            for n in range(3):
+                block(unit, 3 * group + n, n)
+            for n in range(2):
+                other = 2 * group + n
+
+                @pl.when(other == head)
+                def _():
+                    keep(unit, 0).start()
+
+                @pl.when(other != head)
+                def _(other=other):
+                    give(unit, other, 0).start()
+
+            @pl.when(step == 3 - later)
+            def _():
+                for which, (acc, factor) in enumerate(((dk_acc, SCALE), (dv_acc, 1.0))):
+                    back_send[which, unit] = (acc[unit, pl.ds(0, WINDOW_LENGTH)] * factor).astype(jnp.bfloat16)
+
+                @pl.when(has_before & ((ctx != seam) | (unit == last_unit)))
+                def _():
+                    for copy in backs(unit):
+                        copy.start()
+
+                @pl.when((ctx == seam) & (unit < last_unit))
+                def _():
+                    for copy in backs(unit, relayed=True):
+                        copy.start()
+
+            @pl.when((4 * unit + step == rim_unit - 1) & passes_rim)
+            def _():
+                for which, copy in enumerate(rims_onward()):
+                    relay_in(which).wait_recv()
+                    copy.start()
+
+            @pl.when((unit == back_unit + 1) & (step == 2) & passes_back)
+            def _():
+                for which, copy in enumerate(backs_onward()):
+                    relay_in(which).wait_recv()
+                    copy.start()
+
+            @pl.when((unit > lag) & (step == 1 - lag))
+            def _():
+                finish(unit - 1 - lag)
+
+            return carry
+
+        lax.fori_loop(0, 4, one_group, 0)
         return carry
 
     lax.fori_loop(0, units, one_unit, 0)
+    @pl.when(lag > 0)
+    def _():
+        finish(units - 2)
+
     finish(units - 1)
+
+    @pl.when(passes_rim | passes_back)
+    def _():
+        for which in range(2):
+            relay_in(which).wait_send()
 
     def drain(unit, carry):
         @pl.when(has_after)
@@ -331,9 +472,9 @@
                 copy.wait_send()
 
         for which in range(3):
-            exchange(unit, 0, which).wait()
+            keep(unit, which).wait()
             for step in range(1, head_count):
-                exchange(unit, step, which).wait()
+                taken(unit, lax.rem(head + step, head_count), which).wait()
         return carry
 
     lax.fori_loop(0, units, drain, 0)
@@ -353,9 +494,9 @@
     return pl.pallas_call(
         functools.partial(kernel, head_count, ctx_count),
         out_shape=(
-            jax.ShapeDtypeStruct((SLIDING_LAYERS, rows_out, queries.shape[2] * head_count), low),
-            jax.ShapeDtypeStruct((SLIDING_LAYERS, rows_out, keys.shape[2] * head_count), low),
-            jax.ShapeDtypeStruct((SLIDING_LAYERS, rows_out, values.shape[2] * head_count), low),
+            pltpu.VMEM((SLIDING_LAYERS, rows_out, queries.shape[2] * head_count), low),
+            pltpu.VMEM((SLIDING_LAYERS, rows_out, keys.shape[2] * head_count), low),
+            pltpu.VMEM((SLIDING_LAYERS, rows_out, values.shape[2] * head_count), low),
         ),
         in_specs=[
             pl.BlockSpec(memory_space=pltpu.SMEM),
@@ -366,7 +507,7 @@
             anywhere,
             anywhere,
         ],
-        out_specs=(anywhere, anywhere, anywhere),
+        out_specs=(pl.BlockSpec(memory_space=pltpu.VMEM),) * 3,
         scratch_shapes=[
             pltpu.VMEM((units, tokens, pair), low),
             pltpu.VMEM((units, tokens, pair), low),
@@ -375,8 +516,8 @@
             pltpu.VMEM((units, ext, HEAD_SIZE), low),
             pltpu.VMEM((HEAD_SIZE, ext), low),
             pltpu.VMEM((SLIDING_LAYERS, len(BIASED), ROWS, ROWS), wide),
-            pltpu.VMEM((span, 2 * ROWS), low),
-            pltpu.VMEM((span, 2 * ROWS), low),
+            pltpu.VMEM((3, span, 2 * ROWS), low),
+            pltpu.VMEM((3, span, 2 * ROWS), low),
             pltpu.VMEM((units, ext, HEAD_SIZE), wide),
             pltpu.VMEM((units, ext, HEAD_SIZE), wide),
             pltpu.VMEM((units, tokens, pair), low),
@@ -384,6 +525,7 @@
             pltpu.VMEM((units, tokens, HEAD_SIZE), low),
             pltpu.VMEM((2, units, WINDOW_LENGTH, HEAD_SIZE), low),
             pltpu.VMEM((2, units, WINDOW_LENGTH, HEAD_SIZE), low),
+            pltpu.VMEM((2, WINDOW_LENGTH, HEAD_SIZE), low),
             dma((5, units)),
             dma((2, units)),
             dma((2, units)),
@@ -392,9 +534,11 @@
             dma((3, units, head_count)),
             dma((3, units, head_count)),
             dma((3, units)),
+            dma((2,)),
+            dma((2,)),
         ],
         compiler_params=pltpu.CompilerParams(
-            collective_id=0, has_side_effects=True, vmem_limit_bytes=60 * 2**20
+            collective_id=0, has_side_effects=True, vmem_limit_bytes=50 * 2**20
         ),
         name="band_grads",
     )(window, log_norm, queries, keys, values, attn_out, grad_out)

time: 124 us -> 105 us (0.85)
  the two profiles are of different devices: /device:TPU:6 before, /device:TPU:99 now
where the time goes in v2:
time: 105 us
  Pallas kernels  100 us (95%)
  local copies, waits for them, and re-layouts  3.95 us (4%)
    pallas_call x1, Pallas kernels, shards(): pl.pallas_call(functools.partial(kernel, head_count, ctx_count), out_shap...  100 us
    unnamed x3, local copies, waits for them, and re-layouts  3.95 us

profile of v2, /device:TPU:99, one launch (start us, length us, event | category | flops | bytes accessed | tf_op | source)
XLA Modules:
  0.0 105.0 jit_solution(10635810391548117841)
XLA Ops:
  0.6 100.4 %band_grads.1 = (bf16[2,192,4096]{2,1,0:T(8,128)(2,1)S(1)}, bf16[2,192,2048]{2,1,0:T(8,128)(2,1)S(1)}, bf16[2,192,2048]{2,1,0:T(8,128)(2,1)S(1)}) custom-call(s32[2]{0:T(128)} %win_ref.1, f32[2,4,1536]{2,1,0:T(4,128)} %lse_ref.1, bf16[2,1536,512]{2,1,0:T(8,128)(2,1)} %q_hbm.1, bf16[2,1536,256]{2,1,0:T(8,128)(2,1)} %k_hbm.1, bf16[2,1536,256]{2,1,0:T(8,128)(2,1)} %v_hbm.1, ...), custom_call_target="tpu_custom_call" | custom-call | tf_op jit(solution)/shard_map/band_grads/pallas_call | solution.py:494
  101.0 1.7 %copy.13 = bf16[2,192,4096]{2,1,0:T(8,128)(2,1)} copy(bf16[2,192,4096]{2,1,0:T(8,128)(2,1)S(1)} %get-tuple-element.3) | data formatting | bytes 6291456
  102.7 1.1 %copy.14 = bf16[2,192,2048]{2,1,0:T(8,128)(2,1)} copy(bf16[2,192,2048]{2,1,0:T(8,128)(2,1)S(1)} %get-tuple-element.4) | data formatting | bytes 3145728
  103.9 1.1 %copy.15 = bf16[2,192,2048]{2,1,0:T(8,128)(2,1)} copy(bf16[2,192,2048]{2,1,0:T(8,128)(2,1)S(1)} %get-tuple-element.5) | data formatting | bytes 3145728

commit v3 on v2

--- a/solution.py
+++ b/solution.py
@@ -90,6 +90,7 @@
     rim_unit = (ctx + 1) // 2
     back_unit = (ctx - seam - 2) // 2
     last_unit = units - 1
+    late = 1 - ((ctx - seam) * (ctx - seam) + ctx_count * ctx_count - 1) // (ctx_count * ctx_count)
     to_seam = ctx - (seam - 1)
     lag = 1 - (to_seam * to_seam + ctx_count * ctx_count - 1) // (ctx_count * ctx_count)
 
@@ -291,11 +292,11 @@
 
     def turn(unit, lower, upper):
         def step(index, carry):
-            rows = pl.ds(pl.multiple_of(index * ROWS, ROWS), ROWS)
-            k_turned[:, rows] = k_ext[unit, rows].astype(jnp.float32).T.astype(jnp.bfloat16)
+            rows = pl.ds(pl.multiple_of(index * 4 * ROWS, 4 * ROWS), 4 * ROWS)
+            k_turned[:, rows] = k_ext[unit, rows].T
             return carry
 
-        lax.fori_loop(lower, upper, step, 0)
+        lax.fori_loop(lower // 4, upper // 4, step, 0)
 
     def block(unit, index, slot):
         layer, group = place(unit)
@@ -353,14 +354,8 @@
         return lax.rem(head // line + across, 2) * line + lax.rem(lax.rem(head, line) + along, line)
 
     def finish(unit):
-        @pl.when(has_after)
-        def _():
-            for copy in backs(unit):
-                copy.wait_recv()
-
         own = tokens - WINDOW_LENGTH
-        for which, (acc, stage) in enumerate(((dk_acc, dk_stage), (dv_acc, dv_stage))):
-            factor = SCALE if which == 0 else 1.0
+        for which, (acc, stage, factor) in enumerate(((dk_acc, dk_stage, SCALE), (dv_acc, dv_stage, 1.0))):
 
             def step(index, carry, acc=acc, stage=stage, which=which, factor=factor):
                 rows = pl.ds(pl.multiple_of(index * ROWS, ROWS), ROWS)
@@ -370,12 +365,15 @@
                 return carry
 
             stage[unit, pl.ds(0, own)] = (acc[unit, pl.ds(WINDOW_LENGTH, own)] * factor).astype(jnp.bfloat16)
+
+            @pl.when(has_after)
+            def _(which=which):
+                backs(unit)[which].wait_recv()
+
             lax.fori_loop(0, halo_blocks, step, 0)
-        for across, along in ORDER:
-            for which in (1, 2):
-                give(unit, moved_head(across, along), which).start()
-        for which in (1, 2):
-            keep(unit, which).start()
+            for across, along in ORDER:
+                give(unit, moved_head(across, along), which + 1).start()
+            keep(unit, which + 1).start()
 
     def one_unit(unit, carry):
         for copy in loads(unit):
@@ -401,31 +399,29 @@
 
             for n in range(3):
                 block(unit, 3 * group + n, n)
-            for n in range(2):
-                other = 2 * group + n
-
-                @pl.when(other == head)
-                def _():
-                    keep(unit, 0).start()
-
-                @pl.when(other != head)
-                def _(other=other):
-                    give(unit, other, 0).start()
-
             @pl.when(step == 3 - later)
             def _():
                 for which, (acc, factor) in enumerate(((dk_acc, SCALE), (dv_acc, 1.0))):
                     back_send[which, unit] = (acc[unit, pl.ds(0, WINDOW_LENGTH)] * factor).astype(jnp.bfloat16)
 
-                @pl.when(has_before & ((ctx != seam) | (unit == last_unit)))
+                    @pl.when(has_before & ((ctx != seam) | (unit == last_unit)))
+                    def _(which=which):
+                        backs(unit)[which].start()
+
+                    @pl.when((ctx == seam) & (unit < last_unit))
+                    def _(which=which):
+                        backs(unit, relayed=True)[which].start()
+
+            for n in range(2):
+                other = 2 * group + n
+
+                @pl.when(other == head)
                 def _():
-                    for copy in backs(unit):
-                        copy.start()
-
-                @pl.when((ctx == seam) & (unit < last_unit))
-                def _():
-                    for copy in backs(unit, relayed=True):
-                        copy.start()
+                    keep(unit, 0).start()
+
+                @pl.when(other != head)
+                def _(other=other):
+                    give(unit, other, 0).start()
 
             @pl.when((4 * unit + step == rim_unit - 1) & passes_rim)
             def _():
@@ -439,7 +435,7 @@
                     relay_in(which).wait_recv()
                     copy.start()
 
-            @pl.when((unit > lag) & (step == 1 - lag))
+            @pl.when((unit > lag) & (step == 1 - lag + late))
             def _():
                 finish(unit - 1 - lag)
 
@@ -478,6 +474,33 @@
         return carry
 
     lax.fori_loop(0, units, drain, 0)
+
+
+def place_outputs(*refs):
+    count = (len(refs) - 1) // 2
+    copies = [
+        pltpu.make_async_copy(
+            refs[n].at[layer], refs[count + n].at[layer], refs[-1].at[n, layer]
+        )
+        for n in range(count)
+        for layer in range(SLIDING_LAYERS)
+    ]
+    for copy in copies:
+        copy.start()
+    for copy in copies:
+        copy.wait()
+
+
+def placed(arrays):
+    return pl.pallas_call(
+        place_outputs,
+        out_shape=tuple(jax.ShapeDtypeStruct(a.shape, a.dtype) for a in arrays),
+        in_specs=[pl.BlockSpec(memory_space=pltpu.VMEM)] * len(arrays),
+        out_specs=(pl.BlockSpec(memory_space=pl.ANY),) * len(arrays),
+        scratch_shapes=[pltpu.SemaphoreType.DMA((len(arrays), SLIDING_LAYERS))],
+        compiler_params=pltpu.CompilerParams(vmem_limit_bytes=16 * 2**20),
+        name="place_outputs",
+    )(*arrays)
 
 
 def shards(ctx_count, head_count, queries, keys, values, attn_out, grad_out, log_norm, window):
@@ -491,7 +514,7 @@
     low, wide = jnp.bfloat16, jnp.float32
     anywhere = pl.BlockSpec(memory_space=pl.ANY)
     dma = pltpu.SemaphoreType.DMA
-    return pl.pallas_call(
+    results = pl.pallas_call(
         functools.partial(kernel, head_count, ctx_count),
         out_shape=(
             pltpu.VMEM((SLIDING_LAYERS, rows_out, queries.shape[2] * head_count), low),
@@ -542,6 +565,7 @@
         ),
         name="band_grads",
     )(window, log_norm, queries, keys, values, attn_out, grad_out)
+    return placed(results)
 
 
 def solution(mesh):

time: 105 us -> 101 us (0.962)
  the two profiles are of different devices: /device:TPU:99 before, /device:TPU:6 now
where the time goes in v3:
time: 101 us; the launch traced here: 99.4 us
  Pallas kernels  98.8 us (98%)
    pallas_call x1, Pallas kernels, shards(): pl.pallas_call(functools.partial(kernel, head_count, ctx_count), out_shap...  96 us
    pallas_call x1, Pallas kernels, placed(): pl.pallas_call(place_outputs, out_shape=tuple((jax.ShapeDtypeStruct(a.sha...  2.72 us

profile of v3, /device:TPU:6, one launch (start us, length us, event | category | flops | bytes accessed | tf_op | source)
XLA Modules:
  0.0 99.4 jit_solution(17655812386373296793)
XLA Ops:
  0.6 96.0 %band_grads.1 = (bf16[2,192,4096]{2,1,0:T(8,128)(2,1)S(1)}, bf16[2,192,2048]{2,1,0:T(8,128)(2,1)S(1)}, bf16[2,192,2048]{2,1,0:T(8,128)(2,1)S(1)}) custom-call(s32[2]{0:T(128)} %win_ref.1, f32[2,4,1536]{2,1,0:T(4,128)} %lse_ref.1, bf16[2,1536,512]{2,1,0:T(8,128)(2,1)} %q_hbm.1, bf16[2,1536,256]{2,1,0:T(8,128)(2,1)} %k_hbm.1, bf16[2,1536,256]{2,1,0:T(8,128)(2,1)} %v_hbm.1, ...), custom_call_target="tpu_custom_call" | custom-call | tf_op jit(solution)/shard_map/band_grads/pallas_call | solution.py:517
  96.7 2.7 %place_outputs.1 = (bf16[2,192,4096]{2,1,0:T(8,128)(2,1)}, bf16[2,192,2048]{2,1,0:T(8,128)(2,1)}, bf16[2,192,2048]{2,1,0:T(8,128)(2,1)}) custom-call(bf16[2,192,4096]{2,1,0:T(8,128)(2,1)S(1)} %get-tuple-element.6.refs_0_, bf16[2,192,2048]{2,1,0:T(8,128)(2,1)S(1)} %get-tuple-element.7.refs_1_, bf16[2,192,2048]{2,1,0:T(8,128)(2,1)S(1)} %get-tuple-element.8.refs_2_), custom_call_target="tpu_custom_call" | custom-call | tf_op jit(solution)/shard_map/place_outputs/pallas_call | solution.py:495

commit v4 on v3

--- a/solution.py
+++ b/solution.py
@@ -370,7 +370,7 @@
             def _(which=which):
                 backs(unit)[which].wait_recv()
 
-            lax.fori_loop(0, halo_blocks, step, 0)
+            lax.fori_loop(0, halo_blocks, step, 0, unroll=4)
             for across, along in ORDER:
                 give(unit, moved_head(across, along), which + 1).start()
             keep(unit, which + 1).start()
@@ -429,7 +429,7 @@
                     relay_in(which).wait_recv()
                     copy.start()
 
-            @pl.when((unit == back_unit + 1) & (step == 2) & passes_back)
+            @pl.when((unit == back_unit + 1) & (step == 1) & passes_back)
             def _():
                 for which, copy in enumerate(backs_onward()):
                     relay_in(which).wait_recv()

time: 101 us -> 99.6 us (0.986); the launches traced: 99.4 us -> 99.4 us
  no operation moved by 1% of the time
where the time goes in v4:
time: 99.6 us; the launch traced here: 99.4 us
  Pallas kernels  98.8 us (99%)
    pallas_call x1, Pallas kernels, shards(): pl.pallas_call(functools.partial(kernel, head_count, ctx_count), out_shap...  96 us
    pallas_call x1, Pallas kernels, placed(): pl.pallas_call(place_outputs, out_shape=tuple((jax.ShapeDtypeStruct(a.sha...  2.72 us

profile of v4, /device:TPU:6, one launch (start us, length us, event | category | flops | bytes accessed | tf_op | source)
XLA Modules:
  0.0 99.4 jit_solution(3978078219702788689)
XLA Ops:
  0.6 96.0 %band_grads.1 = (bf16[2,192,4096]{2,1,0:T(8,128)(2,1)S(1)}, bf16[2,192,2048]{2,1,0:T(8,128)(2,1)S(1)}, bf16[2,192,2048]{2,1,0:T(8,128)(2,1)S(1)}) custom-call(s32[2]{0:T(128)} %win_ref.1, f32[2,4,1536]{2,1,0:T(4,128)} %lse_ref.1, bf16[2,1536,512]{2,1,0:T(8,128)(2,1)} %q_hbm.1, bf16[2,1536,256]{2,1,0:T(8,128)(2,1)} %k_hbm.1, bf16[2,1536,256]{2,1,0:T(8,128)(2,1)} %v_hbm.1, ...), custom_call_target="tpu_custom_call" | custom-call | tf_op jit(solution)/shard_map/band_grads/pallas_call | solution.py:517
  96.7 2.7 %place_outputs.1 = (bf16[2,192,4096]{2,1,0:T(8,128)(2,1)}, bf16[2,192,2048]{2,1,0:T(8,128)(2,1)}, bf16[2,192,2048]{2,1,0:T(8,128)(2,1)}) custom-call(bf16[2,192,4096]{2,1,0:T(8,128)(2,1)S(1)} %get-tuple-element.6.refs_0_, bf16[2,192,2048]{2,1,0:T(8,128)(2,1)S(1)} %get-tuple-element.7.refs_1_, bf16[2,192,2048]{2,1,0:T(8,128)(2,1)S(1)} %get-tuple-element.8.refs_2_), custom_call_target="tpu_custom_call" | custom-call | tf_op jit(solution)/shard_map/place_outputs/pallas_call | solution.py:495
